TPU v7x, 128 devices: a whole 4x4x4 slice. The times are simulated.
128 devices in a mesh: row: 8 (over y, core), col: 16 (over x, z).
Axes of the slice: x: 4, y: 4, z: 4, core: 2. Of those that a mesh axis runs over, the one named last changes fastest.
Arguments:
- parent_front: float32 [4, 8, 256, 2, 16, 256], P(None, 'row', None, None, 'col'), may hold values from -6 to 48, as said below
- child_tiles: bfloat16 [128, 64, 256, 256], P(('row', 'col')), may hold values from -6 to 6
- tile_target: int32 [128, 64, 2], replicated, may hold values from 0 to 31, as said below
Outputs:
- factored_front: float32 [4, 8, 256, 2, 16, 256], P(None, 'row', None, None, 'col')
Inputs may be any that keep to these rules, and one draw needn't show every extreme that they name: The leading 6 * 256 rows and columns of parent_front form a symmetric matrix with diagonal entries in 32 to 48 and other entries of magnitude at most 30 / 1536. tile_target[d, s] is the parent tile (row, column) into which tile s of device d is added (device d is mesh row d // 16, column d % 16); rows are 6 or more. Parent tile (I, J) lives on mesh row I % 8, column J % 16. The 64 tiles of one device go to 64 different devices, and one device receives a tile from every device.
All inputs are finite; a program needn't handle non-finite values.
Results may differ from a plain program's by a relative error of at most 0.0003.
Values may be sent and summed in bfloat16 or wider, within the bound.
No kernel may reach another device: no remote copies, remote signals or barrier semaphores. Data moves between devices by JAX's collectives and lax.ppermute only.
A program may use at most 192 MiB of HBM per device.

v0:
```python
import jax
import jax.numpy as jnp
from jax import lax
from jax.sharding import PartitionSpec as P

PANELS = 6


def broadcast(shard, axis, root):
    mine = lax.axis_index(axis) == root
    return lax.psum(jnp.where(mine, shard, jnp.zeros_like(shard)), axis)


def shards(parent_front, child_tiles, tile_target):
    lrows = parent_front.shape[0]
    tile = parent_front.shape[2]
    lcols = parent_front.shape[3]
    row_count = lax.axis_size("row")
    col_count = lax.axis_size("col")
    devices = row_count * col_count
    my_row = lax.axis_index("row")
    my_col = lax.axis_index("col")
    myself = my_row * col_count + my_col
    front = parent_front.reshape(lrows, tile, lcols, tile)
    stored = child_tiles.shape[1]
    held = child_tiles.reshape(stored, tile, tile)
    rows_all = tile_target[:, :, 0]
    cols_all = tile_target[:, :, 1]
    owner_all = rows_all % row_count * col_count + cols_all % col_count
    local_all = rows_all // row_count * lcols + cols_all // col_count
    peers = jnp.arange(devices, dtype=jnp.int32)
    my_owner = lax.dynamic_index_in_dim(owner_all, myself, 0, keepdims=False)
    sending = my_owner[None, :] == peers[:, None]
    present = jnp.any(sending, axis=1)
    picked = jnp.sum(jnp.where(sending, jnp.arange(stored, dtype=jnp.int32)[None, :], 0), axis=1)
    outgoing = jnp.where(present[:, None, None], held[picked], jnp.zeros((), jnp.bfloat16))
    arrived = lax.all_to_all(outgoing, ("row", "col"), split_axis=0, concat_axis=0, tiled=True)
    landing = owner_all == myself
    came = jnp.any(landing, axis=1)
    where_to = jnp.sum(jnp.where(landing, local_all, 0), axis=1)
    slots = jnp.arange(lrows * lcols, dtype=jnp.int32)
    onehot = ((where_to[:, None] == slots[None, :]) & came[:, None]).astype(jnp.bfloat16)
    onehot = onehot.reshape(devices, lrows, lcols)
    summed = jnp.einsum("dij,dxy->ixjy", onehot, arrived, preferred_element_type=jnp.float32)
    front = front + summed
    row_ids = my_row + row_count * jnp.arange(lrows, dtype=jnp.int32)
    col_ids = my_col + col_count * jnp.arange(lcols, dtype=jnp.int32)
    stride = col_count // row_count
    pick_rows = my_col // row_count + stride * jnp.arange(lcols, dtype=jnp.int32)
    for step in range(PANELS):
        pivot = broadcast(
            front[step // row_count, :, step // col_count, :], "row", step % row_count
        )
        lower = jnp.linalg.cholesky(pivot)
        column = front[:, :, step // col_count, :].reshape(lrows * tile, tile)
        solved = jax.scipy.linalg.solve_triangular(lower, column.T, lower=True).T.reshape(
            lrows, tile, tile
        )
        factor = jnp.where((row_ids == step)[:, None, None], lower[None, :, :], solved)
        factor = jnp.where((row_ids >= step)[:, None, None], factor, jnp.zeros((), jnp.float32))
        row_panel = broadcast(factor, "col", step % col_count)
        chosen = row_panel[pick_rows]
        col_panel = broadcast(chosen, "row", my_col % row_count)
        update = jnp.einsum("iak,jbk->iajb", row_panel, col_panel, precision=lax.Precision.HIGHEST)
        trailing = front - update
        upper_zero = (row_ids[:, None] == step) & (col_ids[None, :] > step)
        trailing = jnp.where(upper_zero[:, None, :, None], jnp.zeros((), jnp.float32), trailing)
        front = jnp.where(
            (col_ids == step)[None, None, :, None], row_panel[:, :, None, :], trailing
        )
    return front.reshape(parent_front.shape)


def solution(mesh):
    return jax.shard_map(
        shards,
        mesh=mesh,
        in_specs=(
            P(None, "row", None, None, "col", None),
            P(("row", "col"), None, None, None),
            P(),
        ),
        out_specs=P(None, "row", None, None, "col", None),
        check_vma=False,
    )
```

profile of v0, /device:TPU:0, one launch (start us, length us, event | category | flops | bytes accessed | tf_op | source)
XLA Modules:
  0.0 2021.7 jit_solution(16761109816391972855)
XLA Ops:
  8.0 11.5 gather_fusion
  19.5 14.0 broadcast_select_fusion
  33.4 11.7 all-to-all-start
  45.7 4.0 copy.67
  49.8 232.3 %all-to-all-done = bf16[128,256,256]{2,1,0:T(8,128)(2,1)} async-done(((bf16[128,256,256]{2,1,0:T(8,128)(2,1)}), bf16[128,256,256]{2,1,0:T(8,128)(2,1)}, u32[]{:S(2)}, u32[]{:S(2)}) %all-to-all-start) | async-done | bytes 16777248 | tf_op jit(solution)/shard_map/all_to_all | solution.py:37
  282.1 14.8 fusion
  305.7 55.9 %all-reduce.20.cloned.1.call-done = f32[256,256]{0,1:T(8,128)} async-done(((f32[256,256]{0,1:T(8,128)}), f32[256,256]{0,1:T(8,128)}) %all-reduce.20.cloned.1.call-update) | async-done | bytes 262160 | tf_op jit(solution)/shard_map/psum | solution.py:11
  364.4 11.7 cholesky.298
  376.2 9.8 custom-call.21
  388.2 11.7 cholesky.315
  404.3 4.2 while.12
  409.1 20.5 %custom-call.22 = f32[2,128,128]{1,2,0:T(8,128)S(1)} custom-call(f32[2,128,128]{2,1,0:T(8,128)} %copy-done.21), custom_call_target="InvertDiagBlocksLowerTriangular" | custom-call | tf_op jit(solution)/shard_map/jit(_solve_triangular)/triangular_solve | solution.py:56
  435.4 85.3 %all-reduce.22.cloned.1.call-done = f32[4,256,256]{2,1,0:T(8,128)} async-done(((f32[4,256,256]{2,1,0:T(8,128)}), f32[4,256,256]{2,1,0:T(8,128)}) %all-reduce.22.cloned.1.call-update) | async-done | bytes 1048592 | tf_op jit(solution)/shard_map/psum | solution.py:11
  520.7 2.7 gather_fusion.1
  526.8 58.1 %all-reduce.24.cloned.1.call-done = f32[2,256,256]{2,1,0:T(8,128)} async-done(((f32[2,256,256]{2,1,0:T(8,128)}), f32[2,256,256]{2,1,0:T(8,128)}) %all-reduce.24.cloned.1.call-update) | async-done | bytes 524304 | tf_op jit(solution)/shard_map/psum | solution.py:11
  584.9 3.4 select_select_fusion.4
  592.2 57.3 %all-reduce.26.cloned.1.call-done = f32[256,256]{0,1:T(8,128)} async-done(((f32[256,256]{0,1:T(8,128)}), f32[256,256]{0,1:T(8,128)}) %all-reduce.26.cloned.1.call-update) | async-done | bytes 262160 | tf_op jit(solution)/shard_map/psum | solution.py:11
  651.6 11.7 cholesky.332
  663.4 9.8 custom-call.23
  673.7 11.7 cholesky.349
  688.1 4.5 while.13
  692.6 19.7 custom-call.24
  715.9 86.3 %all-reduce.28.cloned.1.call-done = f32[4,256,256]{2,1,0:T(8,128)} async-done(((f32[4,256,256]{2,1,0:T(8,128)}), f32[4,256,256]{2,1,0:T(8,128)}) %all-reduce.28.cloned.1.call-update) | async-done | bytes 1048592 | tf_op jit(solution)/shard_map/psum | solution.py:11
  806.5 58.6 %all-reduce.30.cloned.1.call-done = f32[2,256,256]{2,1,0:T(8,128)} async-done(((f32[2,256,256]{2,1,0:T(8,128)}), f32[2,256,256]{2,1,0:T(8,128)}) %all-reduce.30.cloned.1.call-update) | async-done | bytes 524304 | tf_op jit(solution)/shard_map/psum | solution.py:11
  865.1 4.0 select_select_fusion.3
  873.0 55.9 %all-reduce.32.cloned.1.call-done = f32[256,256]{0,1:T(8,128)} async-done(((f32[256,256]{0,1:T(8,128)}), f32[256,256]{0,1:T(8,128)}) %all-reduce.32.cloned.1.call-update) | async-done | bytes 262160 | tf_op jit(solution)/shard_map/psum | solution.py:11
  931.7 11.7 cholesky.366
  943.5 9.8 custom-call.25
  955.5 11.7 cholesky.383
  970.6 5.5 while.14
  976.8 20.5 %custom-call.26 = f32[2,128,128]{1,2,0:T(8,128)S(1)} custom-call(f32[2,128,128]{2,1,0:T(8,128)} %copy-done.22), custom_call_target="InvertDiagBlocksLowerTriangular" | custom-call | tf_op jit(solution)/shard_map/jit(_solve_triangular)/triangular_solve | solution.py:56
  1003.0 86.3 %all-reduce.34.cloned.1.call-done = f32[4,256,256]{2,1,0:T(8,128)} async-done(((f32[4,256,256]{2,1,0:T(8,128)}), f32[4,256,256]{2,1,0:T(8,128)}) %all-reduce.34.cloned.1.call-update) | async-done | bytes 1048592 | tf_op jit(solution)/shard_map/psum | solution.py:11
  1089.3 2.7 gather_fusion.3
  1095.4 58.1 %all-reduce.36.cloned.1.call-done = f32[2,256,256]{2,1,0:T(8,128)} async-done(((f32[2,256,256]{2,1,0:T(8,128)}), f32[2,256,256]{2,1,0:T(8,128)}) %all-reduce.36.cloned.1.call-update) | async-done | bytes 524304 | tf_op jit(solution)/shard_map/psum | solution.py:11
  1153.5 3.4 select_select_fusion.2
  1160.8 57.3 %all-reduce.38.cloned.1.call-done = f32[256,256]{0,1:T(8,128)} async-done(((f32[256,256]{0,1:T(8,128)}), f32[256,256]{0,1:T(8,128)}) %all-reduce.38.cloned.1.call-update) | async-done | bytes 262160 | tf_op jit(solution)/shard_map/psum | solution.py:11
  1220.2 11.7 cholesky.400
  1232.0 9.8 custom-call.27
  1242.3 11.7 cholesky.417
  1256.7 4.5 while.15
  1261.3 19.7 custom-call.28
  1284.6 86.3 %all-reduce.40.cloned.1.call-done = f32[4,256,256]{2,1,0:T(8,128)} async-done(((f32[4,256,256]{2,1,0:T(8,128)}), f32[4,256,256]{2,1,0:T(8,128)}) %all-reduce.40.cloned.1.call-update) | async-done | bytes 1048592 | tf_op jit(solution)/shard_map/psum | solution.py:11
  1370.9 2.7 gather_fusion.4
  1377.1 58.1 %all-reduce.42.cloned.1.call-done = f32[2,256,256]{2,1,0:T(8,128)} async-done(((f32[2,256,256]{2,1,0:T(8,128)}), f32[2,256,256]{2,1,0:T(8,128)}) %all-reduce.42.cloned.1.call-update) | async-done | bytes 524304 | tf_op jit(solution)/shard_map/psum | solution.py:11
  1435.2 3.4 select_select_fusion.1
  1442.5 57.3 %all-reduce.44.cloned.1.call-done = f32[256,256]{0,1:T(8,128)} async-done(((f32[256,256]{0,1:T(8,128)}), f32[256,256]{0,1:T(8,128)}) %all-reduce.44.cloned.1.call-update) | async-done | bytes 262160 | tf_op jit(solution)/shard_map/psum | solution.py:11
  1502.0 11.7 cholesky.434
  1513.7 9.8 custom-call.29
  1524.0 11.7 cholesky.451
  1538.4 4.3 while.16
  1542.8 19.7 custom-call.30
  1566.1 86.3 %all-reduce.46.cloned.1.call-done = f32[4,256,256]{2,1,0:T(8,128)} async-done(((f32[4,256,256]{2,1,0:T(8,128)}), f32[4,256,256]{2,1,0:T(8,128)}) %all-reduce.46.cloned.1.call-update) | async-done | bytes 1048592 | tf_op jit(solution)/shard_map/psum | solution.py:11
  1656.6 58.6 %all-reduce.48.cloned.1.call-done = f32[2,256,256]{2,1,0:T(8,128)} async-done(((f32[2,256,256]{2,1,0:T(8,128)}), f32[2,256,256]{2,1,0:T(8,128)}) %all-reduce.48.cloned.1.call-update) | async-done | bytes 524304 | tf_op jit(solution)/shard_map/psum | solution.py:11
  1715.2 4.0 select_select_fusion
  1723.2 55.9 %all-reduce.50.cloned.1.call-done = f32[256,256]{0,1:T(8,128)} async-done(((f32[256,256]{0,1:T(8,128)}), f32[256,256]{0,1:T(8,128)}) %all-reduce.50.cloned.1.call-update) | async-done | bytes 262160 | tf_op jit(solution)/shard_map/psum | solution.py:11
  1781.9 11.7 cholesky.468
  1793.7 9.8 custom-call.31
  1805.7 11.7 cholesky.485
  1820.8 5.8 while.17
  1827.2 20.5 %custom-call.32 = f32[2,128,128]{1,2,0:T(8,128)S(1)} custom-call(f32[2,128,128]{2,1,0:T(8,128)} %copy-done.20), custom_call_target="InvertDiagBlocksLowerTriangular" | custom-call | tf_op jit(solution)/shard_map/jit(_solve_triangular)/triangular_solve | solution.py:56
  1853.5 86.3 %all-reduce.52.cloned.1.call-done = f32[4,256,256]{2,1,0:T(8,128)} async-done(((f32[4,256,256]{2,1,0:T(8,128)}), f32[4,256,256]{2,1,0:T(8,128)}) %all-reduce.52.cloned.1.call-update) | async-done | bytes 1048592 | tf_op jit(solution)/shard_map/psum | solution.py:11
  1945.8 58.2 %all-reduce.54.cloned.1.call-done = f32[2,256,256]{2,1,0:T(8,128)} async-done(((f32[2,256,256]{2,1,0:T(8,128)}), f32[2,256,256]{2,1,0:T(8,128)}) %all-reduce.54.cloned.1.call-update) | async-done | bytes 524304 | tf_op jit(solution)/shard_map/psum | solution.py:11
  2004.0 4.7 select_bitcast_fusion
  2008.7 6.0 copy.107
  (309 shorter events, 145.5 us)
Async XLA Ops:
  33.4 12.2 copy-start.10
  33.4 248.6 %all-to-all-start = ((bf16[128,256,256]{2,1,0:T(8,128)(2,1)}), bf16[128,256,256]{2,1,0:T(8,128)(2,1)}, u32[]{:S(2)}, u32[]{:S(2)}) async-start(bf16[128,256,256]{2,1,0:T(8,128)(2,1)} %broadcast_select_fusion), calls=%async_computation | async-start | bytes 33554432 | tf_op jit(solution)/shard_map/all_to_all | solution.py:37
  45.1 316.5 %all-reduce.20.cloned.1.call-start = ((), (), s32[]{:S(2)}) async-start(), calls=%async_computation.1 | async-start | bytes 524288 | tf_op jit(solution)/shard_map/psum | solution.py:11
  302.0 218.7 %all-reduce.22.cloned.1.call-start = ((), (), s32[]{:S(2)}) async-start(), calls=%async_computation.2 | async-start | bytes 2097152 | tf_op jit(solution)/shard_map/psum | solution.py:11
  363.7 0.7 copy-start.17
  399.9 2.0 copy-start.14
  408.5 0.7 copy-start.21
  431.5 2.6 copy-start.12
  435.3 149.6 %all-reduce.24.cloned.1.call-start = ((), (), s32[]{:S(2)}) async-start(), calls=%async_computation.3 | async-start | bytes 1048576 | tf_op jit(solution)/shard_map/psum | solution.py:11
  520.7 4.7 copy-start.4
  525.3 124.2 %all-reduce.26.cloned.1.call-start = ((), (), s32[]{:S(2)}) async-start(), calls=%async_computation.4 | async-start | bytes 524288 | tf_op jit(solution)/shard_map/psum | solution.py:11
  588.3 1.3 copy-start
  590.3 1.2 slice-start
  590.3 211.9 %all-reduce.28.cloned.1.call-start = ((), (), s32[]{:S(2)}) async-start(), calls=%async_computation.5 | async-start | bytes 2097152 | tf_op jit(solution)/shard_map/psum | solution.py:11
  692.6 21.7 %copy-start.23 = (s32[2,2]{1,0:T(2,128)}, s32[2,2]{1,0:T(2,128)S(1)}, u32[]{:S(2)}) copy-start(s32[2,2]{1,0:T(2,128)S(1)} %get-tuple-element.529) | copy-start | bytes 52
  715.9 149.2 %all-reduce.30.cloned.1.call-start = ((), (), s32[]{:S(2)}) async-start(), calls=%async_computation.6 | async-start | bytes 1048576 | tf_op jit(solution)/shard_map/psum | solution.py:11
  802.3 2.9 copy-start.5
  805.0 123.9 %all-reduce.32.cloned.1.call-start = ((), (), s32[]{:S(2)}) async-start(), calls=%async_computation.7 | async-start | bytes 524288 | tf_op jit(solution)/shard_map/psum | solution.py:11
  869.8 219.5 %all-reduce.34.cloned.1.call-start = ((), (), s32[]{:S(2)}) async-start(), calls=%async_computation.8 | async-start | bytes 2097152 | tf_op jit(solution)/shard_map/psum | solution.py:11
  931.0 0.7 copy-start.18
  967.2 2.6 copy-start.15
  976.1 0.7 copy-start.22
  999.1 2.6 copy-start.13
  1003.0 150.6 %all-reduce.36.cloned.1.call-start = ((), (), s32[]{:S(2)}) async-start(), calls=%async_computation.9 | async-start | bytes 1048576 | tf_op jit(solution)/shard_map/psum | solution.py:11
  1089.3 4.7 copy-start.6
  1093.9 124.2 %all-reduce.38.cloned.1.call-start = ((), (), s32[]{:S(2)}) async-start(), calls=%async_computation.10 | async-start | bytes 524288 | tf_op jit(solution)/shard_map/psum | solution.py:11
  1156.9 1.3 copy-start.1
  1158.9 1.2 slice-start.1
  1158.9 211.9 %all-reduce.40.cloned.1.call-start = ((), (), s32[]{:S(2)}) async-start(), calls=%async_computation.11 | async-start | bytes 2097152 | tf_op jit(solution)/shard_map/psum | solution.py:11
  1160.8 95.9 %copy-start.24 = (s32[2,2]{1,0:T(2,128)S(1)}, s32[2,2]{1,0:T(2,128)}, u32[]{:S(2)}) copy-start(s32[2,2]{1,0:T(2,128)} %get-tuple-element.530) | copy-start | bytes 52
  1284.5 150.7 %all-reduce.42.cloned.1.call-start = ((), (), s32[]{:S(2)}) async-start(), calls=%async_computation.12 | async-start | bytes 1048576 | tf_op jit(solution)/shard_map/psum | solution.py:11
  1370.9 4.9 copy-start.7
  1373.6 61.6 %copy-start.2 = (f32[4,256,2,256]{1,3,2,0:T(8,128)S(1)}, f32[4,256,2,256]{1,3,2,0:T(8,128)}, u32[]{:S(2)}) copy-start(f32[4,256,2,256]{1,3,2,0:T(8,128)} %copy-done.1) | copy-start | bytes 6291460
  1375.6 124.2 %all-reduce.44.cloned.1.call-start = ((), (), s32[]{:S(2)}) async-start(), calls=%async_computation.13 | async-start | bytes 524288 | tf_op jit(solution)/shard_map/psum | solution.py:11
  1438.6 1.3 copy-start.3
  1440.6 1.2 slice-start.2
  1440.7 211.7 %all-reduce.46.cloned.1.call-start = ((), (), s32[]{:S(2)}) async-start(), calls=%async_computation.14 | async-start | bytes 2097152 | tf_op jit(solution)/shard_map/psum | solution.py:11
  1542.7 21.7 %copy-start.25 = (s32[2,2]{1,0:T(2,128)}, s32[2,2]{1,0:T(2,128)S(1)}, u32[]{:S(2)}) copy-start(s32[2,2]{1,0:T(2,128)S(1)} %get-tuple-element.532) | copy-start | bytes 52
  1566.0 149.2 %all-reduce.48.cloned.1.call-start = ((), (), s32[]{:S(2)}) async-start(), calls=%async_computation.15 | async-start | bytes 1048576 | tf_op jit(solution)/shard_map/psum | solution.py:11
  1652.4 2.9 copy-start.8
  1655.2 124.0 %all-reduce.50.cloned.1.call-start = ((), (), s32[]{:S(2)}) async-start(), calls=%async_computation.16 | async-start | bytes 524288 | tf_op jit(solution)/shard_map/psum | solution.py:11
  1719.9 219.8 %all-reduce.52.cloned.1.call-start = ((), (), s32[]{:S(2)}) async-start(), calls=%async_computation.17 | async-start | bytes 2097152 | tf_op jit(solution)/shard_map/psum | solution.py:11
  1781.2 0.7 copy-start.19
  1817.4 2.6 copy-start.16
  1826.6 0.7 copy-start.20
  1849.6 2.6 copy-start.11
  1853.4 150.6 %all-reduce.54.cloned.1.call-start = ((), (), s32[]{:S(2)}) async-start(), calls=%async_computation.18 | async-start | bytes 1048576 | tf_op jit(solution)/shard_map/psum | solution.py:11
  1939.8 4.7 copy-start.9
Sparse Core Ops, SparseCore 0:
  302.2 59.4 all-reduce.19
  435.4 85.2 all-reduce.21
  525.4 59.4 all-reduce.23
  590.4 59.0 all-reduce.25
  716.0 86.2 all-reduce.27
  805.2 59.8 all-reduce.29
  869.9 58.9 all-reduce.31
  1003.1 86.2 all-reduce.33
  1094.0 59.4 all-reduce.35
  1159.1 59.0 all-reduce.37
  1284.6 86.2 all-reduce.39
  1375.8 59.4 all-reduce.41
  1440.8 59.0 all-reduce.43
  1566.1 86.2 all-reduce.45
  1655.3 59.8 all-reduce.47
  1720.1 59.0 all-reduce.49
  1853.5 86.2 all-reduce.51
  1944.5 59.4 all-reduce.53
where the time goes:
time: 2030 us; the launch traced here: 2020 us
  waiting for transfers between devices  1440 us (71%)
  other arithmetic  379 us (19%)
  local copies, waits for them, and re-layouts  108 us (5%)
  matrix products  56.6 us (3%)
  between operations  22.6 us (1%)
    psum x18, waiting for transfers between devices, broadcast(): return lax.psum(jnp.where(mine, shard, jnp.zeros_like(shard)), axis)  1210 us
    all_to_all x1, waiting for transfers between devices, shards(): lax.all_to_all(outgoing, ('row', 'col'), split_axis=0, concat_axis=0, til...  232 us
    another operation x41, other arithmetic, shards(): lower = jnp.linalg.cholesky(pivot)  207 us
    another operation x13, other arithmetic, shards(): jax.scipy.linalg.solve_triangular(lower, column.T, lower=True)  124 us
  transfers between devices with their start and end apart: 19, of which 19 were waited for; matrix products, arithmetic and copies ran while one was open for 1% of the time, Pallas kernels for 0%

commit v1 on v0

--- a/solution.py
+++ b/solution.py
@@ -8,7 +8,7 @@
 
 def broadcast(shard, axis, root):
     mine = lax.axis_index(axis) == root
-    return lax.psum(jnp.where(mine, shard, jnp.zeros_like(shard)), axis)
+    return jnp.sum(lax.all_gather(jnp.where(mine, shard, jnp.zeros_like(shard)), axis), axis=0)
 
 
 def shards(parent_front, child_tiles, tile_target):

time: 2030 us -> 1860 us (0.916)
  waiting for transfers between devices: 1440 us -> 1230 us
  other arithmetic: 379 us -> 445 us
  local copies, waits for them, and re-layouts: 108 us -> 82.8 us
    psum x18 -> x0, waiting for transfers between devices: 1210 us -> none  [broadcast(): return lax.psum(jnp.where(mine, shard, jnp.zeros_like(shard)), axis)]
    all_gather x0 -> x18, waiting for transfers between devices: none -> 990 us  [broadcast(): lax.all_gather(jnp.where(mine, shard, jnp.zeros_like(shard)), axis)]
    reduce_sum x0 -> x18, other arithmetic: none -> 69.4 us  [broadcast(): jnp.sum(lax.all_gather(jnp.where(mine, shard, jnp.zeros_like(shard)), axi...]
where the time goes in v1:
time: 1860 us; the launch traced here: 1850 us
  waiting for transfers between devices  1230 us (66%)
  other arithmetic  445 us (24%)
  local copies, waits for them, and re-layouts  82.8 us (4%)
  matrix products  56.7 us (3%)
  between operations  23 us (1%)
    all_gather x18, waiting for transfers between devices, broadcast(): lax.all_gather(jnp.where(mine, shard, jnp.zeros_like(shard)), axis)  990 us
    all_to_all x1, waiting for transfers between devices, shards(): lax.all_to_all(outgoing, ('row', 'col'), split_axis=0, concat_axis=0, til...  236 us
    another operation x41, other arithmetic, shards(): lower = jnp.linalg.cholesky(pivot)  207 us
    another operation x13, other arithmetic, shards(): jax.scipy.linalg.solve_triangular(lower, column.T, lower=True)  121 us
    reduce_sum x18, other arithmetic, broadcast(): jnp.sum(lax.all_gather(jnp.where(mine, shard, jnp.zeros_like(shard)), axi...  69.4 us
  transfers between devices with their start and end apart: 19, of which 19 were waited for; matrix products, arithmetic and copies ran while one was open for 1% of the time, Pallas kernels for 0%

profile of v1, /device:TPU:0, one launch (start us, length us, event | category | flops | bytes accessed | tf_op | source)
XLA Modules:
  0.0 1850.2 jit_solution(13681476094822794583)
XLA Ops:
  8.0 11.5 gather_fusion
  19.5 14.0 broadcast_select_fusion
  33.4 11.7 all-to-all-start
  45.7 236.4 %all-to-all-done = bf16[128,256,256]{2,1,0:T(8,128)(2,1)} async-done(((bf16[128,256,256]{2,1,0:T(8,128)(2,1)}), bf16[128,256,256]{2,1,0:T(8,128)(2,1)}, u32[]{:S(2)}, u32[]{:S(2)}) %all-to-all-start) | async-done | bytes 16777248 | tf_op jit(solution)/shard_map/all_to_all | solution.py:37
  282.1 16.5 bitcast_add_fusion
  300.8 23.9 %all-gather.43.cloned.1.call-done = f32[8,256,1,256]{3,1,2,0:T(8,128)} async-done(((f32[1,256,1,256]{3,1,2,0:T(8,128)}), f32[8,256,1,256]{3,1,2,0:T(8,128)}) %all-gather.43.cloned.1.call-update) | async-done | bytes 2097168 | tf_op jit(solution)/shard_map/all_gather | solution.py:11
  326.6 11.7 cholesky.298
  338.4 9.8 custom-call.21
  348.7 11.7 cholesky.315
  362.6 4.3 while.12
  366.9 19.7 %custom-call.22 = f32[2,128,128]{1,2,0:T(8,128)S(1)} custom-call(f32[2,128,128]{2,1,0:T(8,128)S(1)} %get-tuple-element.45), custom_call_target="InvertDiagBlocksLowerTriangular" | custom-call | tf_op jit(solution)/shard_map/jit(_solve_triangular)/triangular_solve | solution.py:56
  390.2 111.8 %all-gather.31.cloned.1.call-done = f32[16,4,256,256]{3,2,1,0:T(8,128)} async-done(((f32[1,4,256,256]{3,2,1,0:T(8,128)}), f32[16,4,256,256]{3,2,1,0:T(8,128)}) %all-gather.31.cloned.1.call-update) | async-done | bytes 16777232 | tf_op jit(solution)/shard_map/all_gather | solution.py:11
  502.0 7.0 reduce_sum.186
  511.7 30.6 %all-gather.45.cloned.1.call-done = f32[16,256,256]{2,1,0:T(8,128)} async-done(((f32[2,256,256]{2,1,0:T(8,128)}), f32[16,256,256]{2,1,0:T(8,128)}) %all-gather.45.cloned.1.call-update) | async-done | bytes 4194320 | tf_op jit(solution)/shard_map/all_gather | solution.py:11
  544.8 3.5 fusion.27
  552.8 24.0 %all-gather.47.cloned.1.call-done = f32[8,256,1,256]{3,1,2,0:T(8,128)} async-done(((f32[1,256,1,256]{3,1,2,0:T(8,128)}), f32[8,256,1,256]{3,1,2,0:T(8,128)}) %all-gather.47.cloned.1.call-update) | async-done | bytes 2097168 | tf_op jit(solution)/shard_map/all_gather | solution.py:11
  578.7 11.7 cholesky.332
  590.5 9.8 custom-call.23
  600.8 11.7 cholesky.349
  615.2 4.2 while.13
  619.4 19.7 %custom-call.24 = f32[2,128,128]{1,2,0:T(8,128)S(1)} custom-call(f32[2,128,128]{2,1,0:T(8,128)S(1)} %get-tuple-element.46), custom_call_target="InvertDiagBlocksLowerTriangular" | custom-call | tf_op jit(solution)/shard_map/jit(_solve_triangular)/triangular_solve | solution.py:56
  642.7 111.9 %all-gather.33.cloned.1.call-done = f32[16,4,256,256]{3,2,1,0:T(8,128)} async-done(((f32[1,4,256,256]{3,2,1,0:T(8,128)}), f32[16,4,256,256]{3,2,1,0:T(8,128)}) %all-gather.33.cloned.1.call-update) | async-done | bytes 16777232 | tf_op jit(solution)/shard_map/all_gather | solution.py:11
  754.6 7.0 reduce_sum.189
  764.2 30.6 %all-gather.49.cloned.1.call-done = f32[16,256,256]{2,1,0:T(8,128)} async-done(((f32[2,256,256]{2,1,0:T(8,128)}), f32[16,256,256]{2,1,0:T(8,128)}) %all-gather.49.cloned.1.call-update) | async-done | bytes 4194320 | tf_op jit(solution)/shard_map/all_gather | solution.py:11
  797.4 3.5 fusion.25
  807.2 21.9 %all-gather.51.cloned.1.call-done = f32[8,256,1,256]{3,1,2,0:T(8,128)} async-done(((f32[1,256,1,256]{3,1,2,0:T(8,128)}), f32[8,256,1,256]{3,1,2,0:T(8,128)}) %all-gather.51.cloned.1.call-update) | async-done | bytes 2097168 | tf_op jit(solution)/shard_map/all_gather | solution.py:11
  833.4 11.7 cholesky.366
  845.2 9.8 custom-call.25
  857.1 11.7 cholesky.383
  872.3 5.5 while.14
  878.4 20.5 %custom-call.26 = f32[2,128,128]{1,2,0:T(8,128)S(1)} custom-call(f32[2,128,128]{2,1,0:T(8,128)} %copy-done.18), custom_call_target="InvertDiagBlocksLowerTriangular" | custom-call | tf_op jit(solution)/shard_map/jit(_solve_triangular)/triangular_solve | solution.py:56
  904.6 111.9 %all-gather.35.cloned.1.call-done = f32[16,4,256,256]{3,2,1,0:T(8,128)} async-done(((f32[1,4,256,256]{3,2,1,0:T(8,128)}), f32[16,4,256,256]{3,2,1,0:T(8,128)}) %all-gather.35.cloned.1.call-update) | async-done | bytes 16777232 | tf_op jit(solution)/shard_map/all_gather | solution.py:11
  1016.5 7.0 reduce_sum.192
  1029.9 28.2 %all-gather.53.cloned.1.call-done = f32[16,256,256]{2,1,0:T(8,128)} async-done(((f32[2,256,256]{2,1,0:T(8,128)}), f32[16,256,256]{2,1,0:T(8,128)}) %all-gather.53.cloned.1.call-update) | async-done | bytes 4194320 | tf_op jit(solution)/shard_map/all_gather | solution.py:11
  1061.5 4.6 fusion.23
  1071.4 24.2 %all-gather.55.cloned.1.call-done = f32[8,256,1,256]{3,1,2,0:T(8,128)} async-done(((f32[1,256,1,256]{3,1,2,0:T(8,128)}), f32[8,256,1,256]{3,1,2,0:T(8,128)}) %all-gather.55.cloned.1.call-update) | async-done | bytes 2097168 | tf_op jit(solution)/shard_map/all_gather | solution.py:11
  1097.6 11.7 cholesky.400
  1109.3 9.8 custom-call.27
  1119.6 11.7 cholesky.417
  1134.1 4.2 while.15
  1138.3 19.7 %custom-call.28 = f32[2,128,128]{1,2,0:T(8,128)S(1)} custom-call(f32[2,128,128]{2,1,0:T(8,128)S(1)} %get-tuple-element.48), custom_call_target="InvertDiagBlocksLowerTriangular" | custom-call | tf_op jit(solution)/shard_map/jit(_solve_triangular)/triangular_solve | solution.py:56
  1161.6 111.9 %all-gather.37.cloned.1.call-done = f32[16,4,256,256]{3,2,1,0:T(8,128)} async-done(((f32[1,4,256,256]{3,2,1,0:T(8,128)}), f32[16,4,256,256]{3,2,1,0:T(8,128)}) %all-gather.37.cloned.1.call-update) | async-done | bytes 16777232 | tf_op jit(solution)/shard_map/all_gather | solution.py:11
  1273.4 7.0 reduce_sum.195
  1283.1 30.6 %all-gather.57.cloned.1.call-done = f32[16,256,256]{2,1,0:T(8,128)} async-done(((f32[2,256,256]{2,1,0:T(8,128)}), f32[16,256,256]{2,1,0:T(8,128)}) %all-gather.57.cloned.1.call-update) | async-done | bytes 4194320 | tf_op jit(solution)/shard_map/all_gather | solution.py:11
  1324.2 24.0 %all-gather.59.cloned.1.call-done = f32[8,256,1,256]{3,1,2,0:T(8,128)} async-done(((f32[1,256,1,256]{3,1,2,0:T(8,128)}), f32[8,256,1,256]{3,1,2,0:T(8,128)}) %all-gather.59.cloned.1.call-update) | async-done | bytes 2097168 | tf_op jit(solution)/shard_map/all_gather | solution.py:11
  1350.1 11.7 cholesky.434
  1361.9 9.8 custom-call.29
  1372.2 11.7 cholesky.451
  1386.6 4.2 while.16
  1390.9 19.7 %custom-call.30 = f32[2,128,128]{1,2,0:T(8,128)S(1)} custom-call(f32[2,128,128]{2,1,0:T(8,128)S(1)} %get-tuple-element.49), custom_call_target="InvertDiagBlocksLowerTriangular" | custom-call | tf_op jit(solution)/shard_map/jit(_solve_triangular)/triangular_solve | solution.py:56
  1414.2 111.9 %all-gather.39.cloned.1.call-done = f32[16,4,256,256]{3,2,1,0:T(8,128)} async-done(((f32[1,4,256,256]{3,2,1,0:T(8,128)}), f32[16,4,256,256]{3,2,1,0:T(8,128)}) %all-gather.39.cloned.1.call-update) | async-done | bytes 16777232 | tf_op jit(solution)/shard_map/all_gather | solution.py:11
  1526.0 7.0 reduce_sum.198
  1535.7 30.6 %all-gather.61.cloned.1.call-done = f32[16,256,256]{2,1,0:T(8,128)} async-done(((f32[2,256,256]{2,1,0:T(8,128)}), f32[16,256,256]{2,1,0:T(8,128)}) %all-gather.61.cloned.1.call-update) | async-done | bytes 4194320 | tf_op jit(solution)/shard_map/all_gather | solution.py:11
  1578.7 21.9 %all-gather.63.cloned.1.call-done = f32[8,256,1,256]{3,1,2,0:T(8,128)} async-done(((f32[1,256,1,256]{3,1,2,0:T(8,128)}), f32[8,256,1,256]{3,1,2,0:T(8,128)}) %all-gather.63.cloned.1.call-update) | async-done | bytes 2097168 | tf_op jit(solution)/shard_map/all_gather | solution.py:11
  1604.8 11.7 cholesky.468
  1616.6 9.8 custom-call.31
  1628.6 11.7 cholesky.485
  1643.8 5.6 while.17
  1650.1 20.5 %custom-call.32 = f32[2,128,128]{1,2,0:T(8,128)S(1)} custom-call(f32[2,128,128]{2,1,0:T(8,128)} %copy-done.19), custom_call_target="InvertDiagBlocksLowerTriangular" | custom-call | tf_op jit(solution)/shard_map/jit(_solve_triangular)/triangular_solve | solution.py:56
  1676.3 111.9 %all-gather.41.cloned.1.call-done = f32[16,4,256,256]{3,2,1,0:T(8,128)} async-done(((f32[1,4,256,256]{3,2,1,0:T(8,128)}), f32[16,4,256,256]{3,2,1,0:T(8,128)}) %all-gather.41.cloned.1.call-update) | async-done | bytes 16777232 | tf_op jit(solution)/shard_map/all_gather | solution.py:11
  1788.2 7.0 reduce_sum.201
  1801.5 28.2 %all-gather.65.cloned.1.call-done = f32[16,256,256]{2,1,0:T(8,128)} async-done(((f32[2,256,256]{2,1,0:T(8,128)}), f32[16,256,256]{2,1,0:T(8,128)}) %all-gather.65.cloned.1.call-update) | async-done | bytes 4194320 | tf_op jit(solution)/shard_map/all_gather | solution.py:11
  1833.2 4.6 fusion.17
  1839.7 3.5 copy.204
  (339 shorter events, 165.5 us)
Async XLA Ops:
  33.4 248.6 %all-to-all-start = ((bf16[128,256,256]{2,1,0:T(8,128)(2,1)}), bf16[128,256,256]{2,1,0:T(8,128)(2,1)}, u32[]{:S(2)}, u32[]{:S(2)}) async-start(bf16[128,256,256]{2,1,0:T(8,128)(2,1)} %broadcast_select_fusion), calls=%async_computation | async-start | bytes 33554432 | tf_op jit(solution)/shard_map/all_to_all | solution.py:37
  45.1 279.6 %all-gather.43.cloned.1.call-start = ((), (), s32[]{:S(2)}) async-start(), calls=%async_computation.7 | async-start | bytes 2359296 | tf_op jit(solution)/shard_map/all_gather | solution.py:11
  298.6 1.9 copy-start.6
  299.8 202.2 %all-gather.31.cloned.1.call-start = ((), (), s32[]{:S(2)}) async-start(), calls=%async_computation.1 | async-start | bytes 17825792 | tf_op jit(solution)/shard_map/all_gather | solution.py:11
  390.1 152.2 %all-gather.45.cloned.1.call-start = ((), (), s32[]{:S(2)}) async-start(), calls=%async_computation.8 | async-start | bytes 4718592 | tf_op jit(solution)/shard_map/all_gather | solution.py:11
  510.4 66.3 %all-gather.47.cloned.1.call-start = ((), (), s32[]{:S(2)}) async-start(), calls=%async_computation.9 | async-start | bytes 2359296 | tf_op jit(solution)/shard_map/all_gather | solution.py:11
  544.8 3.5 copy-start.7
  550.3 2.2 copy-start.4
  551.5 203.1 %all-gather.33.cloned.1.call-start = ((), (), s32[]{:S(2)}) async-start(), calls=%async_computation.2 | async-start | bytes 17825792 | tf_op jit(solution)/shard_map/all_gather | solution.py:11
  619.4 21.7 %copy-start.20 = (s32[2,2]{1,0:T(2,128)}, s32[2,2]{1,0:T(2,128)S(1)}, u32[]{:S(2)}) copy-start(s32[2,2]{1,0:T(2,128)S(1)} %get-tuple-element.519) | copy-start | bytes 52
  642.6 152.2 %all-gather.49.cloned.1.call-start = ((), (), s32[]{:S(2)}) async-start(), calls=%async_computation.10 | async-start | bytes 4718592 | tf_op jit(solution)/shard_map/all_gather | solution.py:11
  763.0 66.1 %all-gather.51.cloned.1.call-start = ((), (), s32[]{:S(2)}) async-start(), calls=%async_computation.11 | async-start | bytes 2359296 | tf_op jit(solution)/shard_map/all_gather | solution.py:11
  797.4 3.5 copy-start.5
  803.8 212.6 %all-gather.35.cloned.1.call-start = ((), (), s32[]{:S(2)}) async-start(), calls=%async_computation.3 | async-start | bytes 17825792 | tf_op jit(solution)/shard_map/all_gather | solution.py:11
  832.7 0.7 copy-start.16
  868.9 2.6 copy-start.14
  877.7 0.7 copy-start.18
  900.8 2.6 copy-start.13
  904.6 153.5 %all-gather.53.cloned.1.call-start = ((), (), s32[]{:S(2)}) async-start(), calls=%async_computation.12 | async-start | bytes 4718592 | tf_op jit(solution)/shard_map/all_gather | solution.py:11
  1026.7 68.9 %all-gather.55.cloned.1.call-start = ((), (), s32[]{:S(2)}) async-start(), calls=%async_computation.13 | async-start | bytes 2359296 | tf_op jit(solution)/shard_map/all_gather | solution.py:11
  1058.0 3.4 copy-start.9
  1061.5 4.6 copy-start.11
  1068.0 1.3 copy-start
  1069.6 1.3 slice-start
  1070.3 203.1 %all-gather.37.cloned.1.call-start = ((), (), s32[]{:S(2)}) async-start(), calls=%async_computation.4 | async-start | bytes 17825792 | tf_op jit(solution)/shard_map/all_gather | solution.py:11
  1097.4 36.7 %copy-start.21 = (s32[2,2]{1,0:T(2,128)S(1)}, s32[2,2]{1,0:T(2,128)}, u32[]{:S(2)}) copy-start(s32[2,2]{1,0:T(2,128)} %get-tuple-element.520) | copy-start | bytes 52
  1161.5 152.2 %all-gather.57.cloned.1.call-start = ((), (), s32[]{:S(2)}) async-start(), calls=%async_computation.14 | async-start | bytes 4718592 | tf_op jit(solution)/shard_map/all_gather | solution.py:11
  1281.9 66.3 %all-gather.59.cloned.1.call-start = ((), (), s32[]{:S(2)}) async-start(), calls=%async_computation.15 | async-start | bytes 2359296 | tf_op jit(solution)/shard_map/all_gather | solution.py:11
  1316.3 3.5 copy-start.1
  1321.7 2.1 copy-start.2
  1322.9 203.1 %all-gather.39.cloned.1.call-start = ((), (), s32[]{:S(2)}) async-start(), calls=%async_computation.5 | async-start | bytes 17825792 | tf_op jit(solution)/shard_map/all_gather | solution.py:11
  1390.9 21.7 %copy-start.22 = (s32[2,2]{1,0:T(2,128)}, s32[2,2]{1,0:T(2,128)S(1)}, u32[]{:S(2)}) copy-start(s32[2,2]{1,0:T(2,128)S(1)} %get-tuple-element.522) | copy-start | bytes 52
  1414.1 152.2 %all-gather.61.cloned.1.call-start = ((), (), s32[]{:S(2)}) async-start(), calls=%async_computation.16 | async-start | bytes 4718592 | tf_op jit(solution)/shard_map/all_gather | solution.py:11
  1534.5 66.1 %all-gather.63.cloned.1.call-start = ((), (), s32[]{:S(2)}) async-start(), calls=%async_computation.17 | async-start | bytes 2359296 | tf_op jit(solution)/shard_map/all_gather | solution.py:11
  1568.8 3.5 copy-start.3
  1575.3 212.9 %all-gather.41.cloned.1.call-start = ((), (), s32[]{:S(2)}) async-start(), calls=%async_computation.6 | async-start | bytes 17825792 | tf_op jit(solution)/shard_map/all_gather | solution.py:11
  1604.1 0.7 copy-start.17
  1640.3 2.7 copy-start.15
  1649.5 0.7 copy-start.19
  1672.5 2.6 copy-start.12
  1676.3 153.5 %all-gather.65.cloned.1.call-start = ((), (), s32[]{:S(2)}) async-start(), calls=%async_computation.18 | async-start | bytes 4718592 | tf_op jit(solution)/shard_map/all_gather | solution.py:11
  1829.8 3.4 copy-start.8
  1833.2 4.6 copy-start.10
Sparse Core Ops, SparseCore 0:
  299.9 24.7 all-gather.42
  390.2 111.7 all-gather.30
  510.5 31.6 all-gather.44
  551.6 25.0 all-gather.46
  642.8 111.7 all-gather.32
  763.1 31.6 all-gather.48
  803.9 25.1 all-gather.50
  904.7 111.7 all-gather.34
  1026.9 31.1 all-gather.52
  1070.5 25.1 all-gather.54
  1161.6 111.7 all-gather.36
  1282.0 31.6 all-gather.56
  1323.0 25.0 all-gather.58
  1414.2 111.7 all-gather.38
  1534.6 31.6 all-gather.60
  1575.4 25.0 all-gather.62
  1676.4 111.7 all-gather.40
  1798.6 31.1 all-gather.64
